TPU v7x, 32 devices: a whole 2x2x4 slice. The times are simulated.
32 devices in a mesh: dp: 16 (over z, y, x), mp: 2 (over core).
Axes of the slice: x: 2, y: 2, z: 4, core: 2. Of those that a mesh axis runs over, the one named last changes fastest.
Arguments:
- log_rows: bfloat16 [98304, 256], P('dp'), may hold values from -6 to 6
- query_ids: int32 [98304], P('dp'), may hold values from 0 to 191, as said below
- doc_ranks: int32 [98304], P('dp'), may hold values from 0 to 511, as said below
- row_counts: int32 [16, 16], P('dp'), may hold values from 0 to 384, as said below
- list_lengths: int32 [192], P('dp'), may hold values from 64 to 512, as said below
- gains: float32 [192, 512], P('dp'), may hold values from 0.01 to 1
- weight_in: float32 [256, 4096], P(None, 'mp'), may hold values from -0.375 to 0.375
- bias_in: float32 [4096], P('mp'), may hold values from -3 to 3
- weight_out: float32 [4096], P('mp'), may hold values from -0.3 to 0.3
- moment_w: float32 [256, 4096], P(None, 'mp'), may hold values from -0.6 to 0.6
- second_w: float32 [256, 4096], P(None, 'mp'), may hold values from 0.05 to 2
- moment_b: float32 [4096], P('mp'), may hold values from -0.6 to 0.6
- second_b: float32 [4096], P('mp'), may hold values from 0.05 to 2
- moment_o: float32 [4096], P('mp'), may hold values from -0.6 to 0.6
- second_o: float32 [4096], P('mp'), may hold values from 0.05 to 2
Outputs:
- doc_lambdas: float32 [192, 512], P('dp')
- weight_in_next: float32 [256, 4096], P(None, 'mp')
- moment_w_next: float32 [256, 4096], P(None, 'mp')
- second_w_next: float32 [256, 4096], P(None, 'mp')
- bias_in_next: float32 [4096], P('mp')
- moment_b_next: float32 [4096], P('mp')
- second_b_next: float32 [4096], P('mp')
- weight_out_next: float32 [4096], P('mp')
- moment_o_next: float32 [4096], P('mp')
- second_o_next: float32 [4096], P('mp')
Inputs may be any that keep to these rules, and one draw needn't show every extreme that they name: row_counts[s, j] is at most 384; the live rows that all shards hold for owner j number list_lengths summed over owner j's queries j * 12 to j * 12 + 11; some owner receives 384 live rows from every shard. `query_ids`: A live row of the block for owner j belongs to one of owner j's queries; rows that are not live carry arbitrary ids. `doc_ranks`: the live rows of query q carry the ranks 0 to list_lengths[q] - 1, each once; rows that are not live carry arbitrary ranks. `list_lengths`: every owner has a list of 512 documents.
All inputs are finite; a program needn't handle non-finite values.
Results may differ from a plain program's by a relative error of at most 0.0049.
Values may be sent and summed in bfloat16 or wider, within the bound.
A program may use at most 192 MiB of HBM per device.

v0:
```python
import jax
import jax.numpy as jnp
from jax import lax
from jax.sharding import PartitionSpec as P

beta_one = 0.9
beta_two = 0.95
learn_rate = 0.001
adam_eps = 1e-08


def gelu_tanh(values):
    return jax.nn.gelu(values, approximate=True)


def owner_lambdas(score_rows, gain_rows, lengths):
    list_width = gain_rows.shape[1]
    positions = jnp.arange(list_width)
    discount = 1.0 / jnp.log2(2.0 + positions.astype(jnp.float32))
    keep_mask = (positions[None, :] < lengths[:, None]).astype(jnp.float32)

    def per_list(triple):
        row_score, row_gain, row_keep = triple
        delta_s = row_score[:, None] - row_score[None, :]
        delta_g = row_gain[:, None] - row_gain[None, :]
        weight = (
            jnp.abs(discount[:, None] - discount[None, :]) * row_keep[:, None] * row_keep[None, :]
        )
        pair_term = jnp.maximum(delta_g, 0.0) * jax.nn.sigmoid(-delta_s) - jnp.maximum(
            -delta_g, 0.0
        ) * jax.nn.sigmoid(delta_s)
        return -jnp.sum(weight * pair_term, axis=1)

    return lax.map(per_list, (score_rows, gain_rows, keep_mask))


def adam_step(weights, moment, second, gradient):
    moment_next = beta_one * moment + (1.0 - beta_one) * gradient
    second_next = beta_two * second + (1.0 - beta_two) * gradient * gradient
    weights_next = weights - learn_rate * moment_next / (jnp.sqrt(second_next) + adam_eps)
    return (weights_next, moment_next, second_next)


def per_device(
    log_rows,
    query_ids,
    doc_ranks,
    row_counts,
    list_lengths,
    gains,
    weight_in,
    bias_in,
    weight_out,
    moment_w,
    second_w,
    moment_b,
    second_b,
    moment_o,
    second_o,
):
    shard_count = lax.axis_size("dp")
    features = log_rows.shape[1]
    slot_count = log_rows.shape[0] // shard_count
    list_count, list_width = gains.shape
    owner_rows = list_count * list_width
    query_total = list_count * shard_count
    blocks = log_rows.reshape(shard_count, slot_count, features)
    is_live = jnp.arange(slot_count)[None, :] < row_counts.reshape(shard_count, 1)
    targets = jnp.where(
        is_live,
        query_ids.reshape(shard_count, slot_count) % list_count * list_width
        + doc_ranks.reshape(shard_count, slot_count),
        owner_rows,
    )
    w_low = weight_in.astype(jnp.bfloat16)
    arrived = lax.all_to_all(blocks, "dp", split_axis=0, concat_axis=0, tiled=True)
    arrived_slots = lax.all_to_all(targets, "dp", split_axis=0, concat_axis=0, tiled=True)
    used_rows = (
        jnp.zeros((owner_rows, features), jnp.bfloat16)
        .at[arrived_slots.reshape(-1)]
        .set(arrived.reshape(-1, features), mode="drop")
    )
    pre_act = jnp.dot(used_rows, w_low, preferred_element_type=jnp.float32) + bias_in
    hidden, gelu_back = jax.vjp(gelu_tanh, pre_act)
    scores = lax.psum(jnp.sum(hidden * weight_out, axis=1), "mp")
    lambdas = owner_lambdas(scores.reshape(list_count, list_width), gains, list_lengths)
    row_lambdas = lambdas.reshape(-1) / query_total
    grad_pre = gelu_back(row_lambdas[:, None] * weight_out)[0]
    grad_w = lax.dot_general(
        used_rows,
        grad_pre.astype(jnp.bfloat16),
        (((0,), (0,)), ((), ())),
        preferred_element_type=jnp.float32,
    )
    grad_b = jnp.sum(grad_pre, axis=0)
    grad_o = jnp.sum(row_lambdas[:, None] * hidden, axis=0)
    grad_w, grad_b, grad_o = lax.psum((grad_w, grad_b, grad_o), "dp")
    weight_next, moment_w_next, second_w_next = adam_step(weight_in, moment_w, second_w, grad_w)
    bias_next, moment_b_next, second_b_next = adam_step(bias_in, moment_b, second_b, grad_b)
    out_next, moment_o_next, second_o_next = adam_step(weight_out, moment_o, second_o, grad_o)
    return (
        lambdas,
        weight_next,
        moment_w_next,
        second_w_next,
        bias_next,
        moment_b_next,
        second_b_next,
        out_next,
        moment_o_next,
        second_o_next,
    )


def solution(mesh):
    placed = (
        P("dp", None),
        P("dp"),
        P("dp"),
        P("dp", None),
        P("dp"),
        P("dp", None),
        P(None, "mp"),
        P("mp"),
        P("mp"),
        P(None, "mp"),
        P(None, "mp"),
        P("mp"),
        P("mp"),
        P("mp"),
        P("mp"),
    )
    return jax.shard_map(
        per_device,
        mesh=mesh,
        in_specs=placed,
        out_specs=(
            P("dp", None),
            P(None, "mp"),
            P(None, "mp"),
            P(None, "mp"),
            P("mp"),
            P("mp"),
            P("mp"),
            P("mp"),
            P("mp"),
            P("mp"),
        ),
        check_vma=False,
    )
```

profile of v0, /device:TPU:0, one launch (start us, length us, event | category | flops | bytes accessed | tf_op | source)
XLA Modules:
  0.0 381.7 jit_solution(12026352199556250524)
XLA Ops:
  8.8 15.5 %all_to_all.11 = s32[16,1,384]{2,1,0:T(1,128)S(1)} all-to-all(s32[16,1,384]{2,1,0:T(1,128)S(1)} %compare_select_fusion.1), channel_id=1, replica_groups=mesh['dp'=16,'mp'=2] {'dp'}, dimensions={0} | all-to-all | bytes 49152 | tf_op jit(solution)/shard_map/all_to_all | solution.py:77
  24.2 3.7 all-to-all-start.1
  28.8 59.5 %all-to-all-done.1 = bf16[16,384,256]{2,1,0:T(8,128)(2,1)S(1)} async-done(((bf16[16,384,256]{2,1,0:T(8,128)(2,1)}), bf16[16,384,256]{2,1,0:T(8,128)(2,1)S(1)}, u32[]{:S(2)}, u32[]{:S(2)}) %all-to-all-start.1) | async-done | bytes 3145760 | tf_op jit(solution)/shard_map/all_to_all | solution.py:76
  88.3 1.7 copy-done
  89.9 27.8 %scatter_custom_fusion = bf16[6144,256]{1,0:T(8,128)(2,1)S(1)} fusion(s32[6144]{0:T(1024)S(1)} %bitcast.31, bf16[6144,256]{1,0:T(8,128)(2,1)} %bitcast.24, bf16[]{:T(256)} %constant.12.clone.1), kind=kCustom, calls=%fused_computation.43 | custom fusion | bytes 3146240 | tf_op jit(solution)/shard_map/scatter | solution.py:81
  117.8 26.4 %multiply_reduce_fusion.1 = (f32[6144]{0:T(1024)S(1)}, f32[6144,2048]{1,0:T(8,128)}) fusion(f32[2048]{0:T(1024)} %param.25, f32[2048]{0:T(1024)} %param.24, bf16[6144,256]{1,0:T(8,128)(2,1)S(1)} %scatter_custom_fusion, f32[256,2048]{1,0:T(8,128)} %param.23), kind=kOutput, calls=%fused_computation.35 | convolution fusion | flops 6581381120 | bytes 55615488 | tf_op jit(solution)/shard_map/dot_general | solution.py:83
  144.2 3.6 psum.28
  147.7 23.0 %while.11 = (s32[]{:T(128)}, f32[12,512]{1,0:T(8,128)S(1)}, f32[12,512]{1,0:T(8,128)S(1)}, f32[12,512]{1,0:T(8,128)}, f32[12,512]{1,0:T(8,128)S(1)}, /*index=5*/s32[]{:T(128)}, s32[]{:T(128)}) while((s32[]{:T(128)}, f32[12,512]{1,0:T(8,128)S(1)}, f32[12,512]{1,0:T(8,128)S(1)}, f32[12,512]{1,0:T(8,128)}, f32[12,512]{1,0:T(8,128)S(1)}, ...), condition=%wide.region_5.6_spmd.clone, body=%wide.region_3.5_spmd.clone.sunk | while | flops 4982786 | bytes 32865 | solution.py:34
  148.5 1.1 fusion.43
  150.4 1.1 fusion.43
  152.3 1.1 fusion.43
  154.3 1.1 fusion.43
  156.2 1.1 fusion.43
  158.1 1.1 fusion.43
  160.0 1.1 fusion.43
  163.8 1.1 fusion.43
  165.7 1.1 fusion.43
  167.7 1.1 fusion.43
  169.6 1.1 fusion.43
  170.8 48.6 %fusion.36 = (f32[2048]{0:T(1024)S(1)}, bf16[6144,2048]{1,0:T(8,128)(2,1)}, f32[2048]{0:T(1024)S(1)}) fusion(f32[6144,2048]{1,0:T(8,128)} %get-tuple-element.82, f32[2048]{0:T(1024)S(1)} %copy-done.2, f32[2048]{0:T(1024)S(1)} %copy-done.1, f32[6144]{0:T(1024)S(1)} %div.33), kind=kLoop, calls=%fused_computation.64 | loop fusion | flops 327151616 | bytes 75554816 | tf_op jit(solution)/shard_map/reduce_sum | solution.py:95
  219.5 12.9 %fusion.22 = f32[256,2048]{1,0:T(8,128)} fusion(bf16[6144,256]{1,0:T(8,128)(2,1)S(1)} %scatter_custom_fusion, bf16[6144,2048]{1,0:T(8,128)(2,1)} %get-tuple-element.74), kind=kOutput, calls=%fused_computation.37 | convolution fusion | flops 6442450944 | bytes 30408704 | tf_op jit(solution)/shard_map/dot_general | solution.py:89
  232.4 84.9 %all-reduce = (f32[2048]{0:T(1024)S(1)}, f32[2048]{0:T(1024)S(1)}) all-reduce(f32[2048]{0:T(1024)S(1)} %get-tuple-element.73, f32[2048]{0:T(1024)S(1)} %get-tuple-element.80), channel_id=1, replica_groups=mesh['dp'=16,'mp'=2] {'dp'}, use_global_device_ids=true, to_apply=%region_8.9 | all-reduce | flops 4096 | bytes 32768 | tf_op jit(solution)/shard_map/psum | solution.py:97
  318.0 49.5 %all-reduce.3.cloned.1.call-done = f32[256,2048]{1,0:T(8,128)} async-done(((f32[256,2048]{1,0:T(8,128)}), f32[256,2048]{1,0:T(8,128)}) %all-reduce.3.cloned.1.call-update) | async-done | bytes 2097168 | tf_op jit(solution)/shard_map/psum | solution.py:97
  367.5 7.4 %divide_subtract_fusion = (f32[256,2048]{1,0:T(8,128)}, f32[256,2048]{1,0:T(8,128)}, f32[256,2048]{1,0:T(8,128)}) fusion(f32[256,2048]{1,0:T(8,128)} %param.23, f32[256,2048]{1,0:T(8,128)} %all-reduce.3.cloned.1.call-done, f32[256,2048]{1,0:T(8,128)} %param.26, f32[256,2048]{1,0:T(8,128)} %param.27), kind=kLoop, calls=%fused_computation.41 | loop fusion | flops 5767168 | bytes 14680064 | tf_op jit(solution)/shard_map/sub | solution.py:40
  (87 shorter events, 13.9 us)
Async XLA Ops:
  24.2 64.0 %all-to-all-start.1 = ((bf16[16,384,256]{2,1,0:T(8,128)(2,1)}), bf16[16,384,256]{2,1,0:T(8,128)(2,1)S(1)}, u32[]{:S(2)}, u32[]{:S(2)}) async-start(bf16[16,384,256]{2,1,0:T(8,128)(2,1)} %bitcast.23), calls=%async_computation.1 | async-start | bytes 6291456 | tf_op jit(solution)/shard_map/all_to_all | solution.py:76
  28.0 339.5 %all-reduce.3.cloned.1.call-start = ((), (), s32[]{:S(2)}) async-start(), calls=%async_computation.2 | async-start | bytes 4194304 | tf_op jit(solution)/shard_map/psum | solution.py:97
  88.3 1.7 copy-start
  117.8 53.0 %copy-start.1 = (f32[2048]{0:T(1024)S(1)}, f32[2048]{0:T(1024)}, u32[]{:S(2)}) copy-start(f32[2048]{0:T(1024)} %param.25) | copy-start | bytes 24580
  117.8 53.0 %copy-start.2 = (f32[2048]{0:T(1024)S(1)}, f32[2048]{0:T(1024)}, u32[]{:S(2)}) copy-start(f32[2048]{0:T(1024)} %param.24) | copy-start | bytes 24580
  170.7 48.7 %copy-start.3 = (f32[12,512]{1,0:T(8,128)}, f32[12,512]{1,0:T(8,128)S(1)}, u32[]{:S(2)}) copy-start(f32[12,512]{1,0:T(8,128)S(1)} %get-tuple-element.32) | copy-start | bytes 73732
  219.4 98.0 %copy-start.4 = (f32[2048]{0:T(1024)S(1)}, f32[2048]{0:T(1024)}, u32[]{:S(2)}) copy-start(f32[2048]{0:T(1024)} %param.30) | copy-start | bytes 24580
  219.4 97.9 %copy-start.5 = (f32[2048]{0:T(1024)S(1)}, f32[2048]{0:T(1024)}, u32[]{:S(2)}) copy-start(f32[2048]{0:T(1024)} %param.31) | copy-start | bytes 24580
  219.4 97.9 %copy-start.6 = (f32[2048]{0:T(1024)S(1)}, f32[2048]{0:T(1024)}, u32[]{:S(2)}) copy-start(f32[2048]{0:T(1024)} %param.29) | copy-start | bytes 24580
  219.4 97.9 %copy-start.7 = (f32[2048]{0:T(1024)S(1)}, f32[2048]{0:T(1024)}, u32[]{:S(2)}) copy-start(f32[2048]{0:T(1024)} %param.28) | copy-start | bytes 24580
Sparse Core Ops, SparseCore 0:
  232.5 134.8 all-reduce.2
where the time goes:
time: 383 us; the launch traced here: 382 us
  waiting for transfers between devices  109 us (28%)
  blocking collectives  104 us (27%)
  other arithmetic  71.8 us (19%)
  matrix products  39.3 us (10%)
  local copies, waits for them, and re-layouts  39.2 us (10%)
  between operations  14.2 us (4%)
    psum x1, blocking collectives, per_device(): grad_w, grad_b, grad_o = lax.psum((grad_w, grad_b, grad_o), 'dp')  84.9 us
    all_to_all x1, waiting for transfers between devices, per_device(): lax.all_to_all(blocks, 'dp', split_axis=0, concat_axis=0, tiled=True)  59.5 us
    psum x1, waiting for transfers between devices, per_device(): grad_w, grad_b, grad_o = lax.psum((grad_w, grad_b, grad_o), 'dp')  49.5 us
    reduce_sum x1, other arithmetic, per_device(): grad_b = jnp.sum(grad_pre, axis=0)  48.6 us
    scatter x1, local copies, waits for them, and re-layouts, per_device(): used_rows = jnp.zeros((owner_rows, features), jnp.bfloat16).at[arrived_sl...  27.8 us
    dot_general x1, matrix products, per_device(): jnp.dot(used_rows, w_low, preferred_element_type=jnp.float32) + bias_in  26.4 us
    all_to_all x1, blocking collectives, per_device(): lax.all_to_all(targets, 'dp', split_axis=0, concat_axis=0, tiled=True)  15.5 us
    dot_general x1, matrix products, per_device(): lax.dot_general(used_rows, grad_pre.astype(jnp.bfloat16), (((0,), (0,)),...  12.9 us
  transfers between devices with their start and end apart: 2, of which 2 were waited for; matrix products, arithmetic and copies ran while one was open for 0% of the time, Pallas kernels for 0%

commit v1 on v0

--- a/solution.py
+++ b/solution.py
@@ -1,3 +1,4 @@
+import functools
 import jax
 import jax.numpy as jnp
 from jax import lax
@@ -7,6 +8,31 @@
 beta_two = 0.95
 learn_rate = 0.001
 adam_eps = 1e-08
+
+
+def report_surface(local_x, axis_key):
+    opened = jax.lax.axis_size(axis_key)
+    b_now, vec_out = (opened, jax.lax.axis_index(axis_key))
+    arr_now = local_x.shape[0] // b_now
+    b_next = list(local_x.shape)
+    b_next[0] = arr_now
+    z1 = b_next[0]
+    b_next[0] = z1 * b_now
+    inter = jnp.zeros(b_next, local_x.dtype)
+    for dev_i in range(b_now):
+        current_value = lax.dynamic_slice_in_dim(
+            local_x, (vec_out ^ dev_i) * arr_now, arr_now, axis=0
+        )
+        if dev_i:
+            e_next = tuple(((pp, pp ^ dev_i) for pp in range(b_now)))
+            current_value = jax.lax.ppermute(current_value, axis_key, e_next)
+        inter = lax.dynamic_update_slice_in_dim(
+            inter, current_value, (vec_out ^ dev_i) * z1, axis=0
+        )
+    return inter
+
+
+load_quarters_now = functools.partial(report_surface, axis_key="dp")
 
 
 def gelu_tanh(values):
@@ -73,7 +99,7 @@
         owner_rows,
     )
     w_low = weight_in.astype(jnp.bfloat16)
-    arrived = lax.all_to_all(blocks, "dp", split_axis=0, concat_axis=0, tiled=True)
+    arrived = load_quarters_now(blocks)
     arrived_slots = lax.all_to_all(targets, "dp", split_axis=0, concat_axis=0, tiled=True)
     used_rows = (
         jnp.zeros((owner_rows, features), jnp.bfloat16)

time: 383 us -> 399 us (1.042)
  starting transfers between devices: 3.78 us -> 33.3 us
  blocking collectives: 104 us -> 79.5 us
  local copies, waits for them, and re-layouts: 39.2 us -> 60 us
  waiting for transfers between devices: 109 us -> 96.1 us
    all_to_all x1, waiting for transfers between devices: 59.5 us -> 0.01 us  [per_device(): lax.all_to_all(targets, 'dp', split_axis=0, concat_axis=0, tiled=True)]
    ppermute x0 -> x15, waiting for transfers between devices: none -> 46.2 us  [report_surface(): current_value = jax.lax.ppermute(current_value, axis_key, e_next)]
    ppermute x0 -> x15, starting transfers between devices: none -> 24.9 us  [report_surface(): current_value = jax.lax.ppermute(current_value, axis_key, e_next)]
    all_to_all x1 -> x0, blocking collectives: 15.5 us -> none  [per_device(): lax.all_to_all(targets, 'dp', split_axis=0, concat_axis=0, tiled=True)]
    dynamic_update_slice x0 -> x15, local copies, waits for them, and re-layouts: none -> 10.4 us  [report_surface(): lax.dynamic_update_slice_in_dim(inter, current_value, (vec_out ^ dev_i) *...]
    psum x1, blocking collectives: 84.9 us -> 75.9 us  [per_device(): grad_w, grad_b, grad_o = lax.psum((grad_w, grad_b, grad_o), 'dp')]
    dynamic_slice x24, local copies, waits for them, and re-layouts: 8.89 us -> 17.5 us  [owner_lambdas(): return lax.map(per_list, (score_rows, gain_rows, keep_mask))]
    all_to_all x1, starting transfers between devices: 3.74 us -> 8.36 us  [per_device(): lax.all_to_all(targets, 'dp', split_axis=0, concat_axis=0, tiled=True)]
  transfers between devices with their start and end apart: 2 -> 17, of which waited for: 2 -> 10; matrix products, arithmetic and copies ran while one was open for 0% -> 4% of each run, Pallas kernels for 0% -> 0%
where the time goes in v1:
time: 399 us; the launch traced here: 396 us
  waiting for transfers between devices  96.1 us (24%)
  blocking collectives  79.5 us (20%)
  other arithmetic  73.1 us (18%)
  local copies, waits for them, and re-layouts  60 us (15%)
  matrix products  39.4 us (10%)
  starting transfers between devices  33.3 us (8%)
  between operations  14.3 us (4%)
    psum x1, blocking collectives, per_device(): grad_w, grad_b, grad_o = lax.psum((grad_w, grad_b, grad_o), 'dp')  75.9 us
    psum x1, waiting for transfers between devices, per_device(): grad_w, grad_b, grad_o = lax.psum((grad_w, grad_b, grad_o), 'dp')  49.9 us
    reduce_sum x1, other arithmetic, per_device(): grad_b = jnp.sum(grad_pre, axis=0)  48.7 us
    ppermute x15, waiting for transfers between devices, report_surface(): current_value = jax.lax.ppermute(current_value, axis_key, e_next)  46.2 us
    scatter x1, local copies, waits for them, and re-layouts, per_device(): used_rows = jnp.zeros((owner_rows, features), jnp.bfloat16).at[arrived_sl...  27.8 us
    dot_general x1, matrix products, per_device(): jnp.dot(used_rows, w_low, preferred_element_type=jnp.float32) + bias_in  26.4 us
    ppermute x15, starting transfers between devices, report_surface(): current_value = jax.lax.ppermute(current_value, axis_key, e_next)  24.9 us
    dynamic_slice x24, local copies, waits for them, and re-layouts, owner_lambdas(): return lax.map(per_list, (score_rows, gain_rows, keep_mask))  17.5 us
  transfers between devices with their start and end apart: 17, of which 10 were waited for; matrix products, arithmetic and copies ran while one was open for 4% of the time, Pallas kernels for 0%

profile of v1, /device:TPU:0, one launch (start us, length us, event | category | flops | bytes accessed | tf_op | source)
XLA Modules:
  0.0 396.1 jit_solution(1277744171547035305)
XLA Ops:
  9.6 8.4 %all-to-all-start = ((s32[16,1,384]{2,1,0:T(1,128)}), s32[16,1,384]{2,1,0:T(1,128)}, u32[]{:S(2)}, u32[]{:S(2)}) async-start(s32[16,1,384]{2,1,0:T(1,128)} %compare_select_fusion.1), calls=%async_computation | async-start | bytes 49152 | tf_op jit(solution)/shard_map/all_to_all | solution.py:103
  19.9 1.6 copy-done.1
  21.6 5.5 %collective-permute-start.14 = (bf16[1,384,256]{2,1,0:T(8,128)(2,1)S(1)}, bf16[1,384,256]{2,1,0:T(8,128)(2,1)S(1)}, u32[]{:S(2)}, u32[]{:S(2)}) collective-permute-start(bf16[1,384,256]{2,1,0:T(8,128)(2,1)S(1)} %get-tuple-element.81), channel_id=1, source_target_pairs={{0,30},{2,28},{4,26},{6,24},{8,22},{10,20},{12,18},{14,16},{16,14}... | collective-permute-start | bytes 589832 | tf_op jit(solution)/shard_map/ppermute | solution.py:28
  27.6 3.3 collective-permute-start.12
  35.8 7.3 %collective-permute-done = bf16[1,384,256]{2,1,0:T(8,128)(2,1)S(1)} collective-permute-done((bf16[1,384,256]{2,1,0:T(8,128)(2,1)}, bf16[1,384,256]{2,1,0:T(8,128)(2,1)S(1)}, u32[]{:S(2)}, u32[]{:S(2)}) %collective-permute-start) | collective-permute-done | bytes 196640 | tf_op jit(solution)/shard_map/ppermute | solution.py:28
  45.9 6.2 %collective-permute-done.2 = bf16[1,384,256]{2,1,0:T(8,128)(2,1)S(1)} collective-permute-done((bf16[1,384,256]{2,1,0:T(8,128)(2,1)}, bf16[1,384,256]{2,1,0:T(8,128)(2,1)S(1)}, u32[]{:S(2)}, u32[]{:S(2)}) %collective-permute-start.2) | collective-permute-done | bytes 196640 | tf_op jit(solution)/shard_map/ppermute | solution.py:28
  52.1 3.4 collective-permute-start.4
  56.9 4.8 %collective-permute-done.4 = bf16[1,384,256]{2,1,0:T(8,128)(2,1)S(1)} collective-permute-done((bf16[1,384,256]{2,1,0:T(8,128)(2,1)}, bf16[1,384,256]{2,1,0:T(8,128)(2,1)S(1)}, u32[]{:S(2)}, u32[]{:S(2)}) %collective-permute-start.4) | collective-permute-done | bytes 196640 | tf_op jit(solution)/shard_map/ppermute | solution.py:28
  64.6 6.4 %collective-permute-done.6 = bf16[1,384,256]{2,1,0:T(8,128)(2,1)S(1)} collective-permute-done((bf16[1,384,256]{2,1,0:T(8,128)(2,1)}, bf16[1,384,256]{2,1,0:T(8,128)(2,1)S(1)}, u32[]{:S(2)}, u32[]{:S(2)}) %collective-permute-start.6) | collective-permute-done | bytes 196640 | tf_op jit(solution)/shard_map/ppermute | solution.py:28
  71.7 5.4 %collective-permute-done.7 = bf16[1,384,256]{2,1,0:T(8,128)(2,1)S(1)} collective-permute-done((bf16[1,384,256]{2,1,0:T(8,128)(2,1)}, bf16[1,384,256]{2,1,0:T(8,128)(2,1)S(1)}, u32[]{:S(2)}, u32[]{:S(2)}) %collective-permute-start.7) | collective-permute-done | bytes 196640 | tf_op jit(solution)/shard_map/ppermute | solution.py:28
  77.1 3.0 collective-permute-start.9
  80.8 6.8 %collective-permute-done.8 = bf16[1,384,256]{2,1,0:T(8,128)(2,1)S(1)} collective-permute-done((bf16[1,384,256]{2,1,0:T(8,128)(2,1)}, bf16[1,384,256]{2,1,0:T(8,128)(2,1)S(1)}, u32[]{:S(2)}, u32[]{:S(2)}) %collective-permute-start.8) | collective-permute-done | bytes 196640 | tf_op jit(solution)/shard_map/ppermute | solution.py:28
  88.4 5.3 %collective-permute-done.9 = bf16[1,384,256]{2,1,0:T(8,128)(2,1)S(1)} collective-permute-done((bf16[1,384,256]{2,1,0:T(8,128)(2,1)}, bf16[1,384,256]{2,1,0:T(8,128)(2,1)S(1)}, u32[]{:S(2)}, u32[]{:S(2)}) %collective-permute-start.9) | collective-permute-done | bytes 196640 | tf_op jit(solution)/shard_map/ppermute | solution.py:28
  93.7 4.9 %collective-permute-start.11 = (bf16[1,384,256]{2,1,0:T(8,128)(2,1)S(1)}, bf16[1,384,256]{2,1,0:T(8,128)(2,1)S(1)}, u32[]{:S(2)}, u32[]{:S(2)}) collective-permute-start(bf16[1,384,256]{2,1,0:T(8,128)(2,1)S(1)} %copy-done.3), channel_id=1, source_target_pairs={{0,24},{2,26},{4,28},{6,30},{8,16},{10,18},{12,20},{14,22},{16,8},... | collective-permute-start | bytes 589832 | tf_op jit(solution)/shard_map/ppermute | solution.py:28
  100.0 2.4 collective-permute-done.11
  105.2 27.8 %scatter_custom_fusion = bf16[6144,256]{1,0:T(8,128)(2,1)S(1)} fusion(s32[6144]{0:T(1024)} %bitcast.30, bf16[6144,256]{1,0:T(8,128)(2,1)} %bitcast.24, bf16[]{:T(256)} %constant.50.clone.1), kind=kCustom, calls=%fused_computation.43 | custom fusion | bytes 3146240 | tf_op jit(solution)/shard_map/scatter | solution.py:107
  133.0 26.4 %multiply_reduce_fusion.1 = (f32[6144]{0:T(1024)S(1)}, f32[6144,2048]{1,0:T(8,128)}) fusion(f32[2048]{0:T(1024)S(1)} %copy-done.5, f32[2048]{0:T(1024)S(1)} %copy-done.6, bf16[6144,256]{1,0:T(8,128)(2,1)S(1)} %scatter_custom_fusion, f32[256,2048]{1,0:T(8,128)} %param.23), kind=kOutput, calls=%fused_computation.35 | convolution fusion | flops 6581381120 | bytes 55615488 | tf_op jit(solution)/shard_map/dot_general | solution.py:109
  159.4 3.6 psum.28
  163.0 31.5 %while.11 = (s32[]{:T(128)}, f32[12,512]{1,0:T(8,128)S(1)}, f32[12,512]{1,0:T(8,128)}, f32[12,512]{1,0:T(8,128)}, f32[12,512]{1,0:T(8,128)S(1)}, /*index=5*/s32[]{:T(128)}, s32[]{:T(128)}) while((s32[]{:T(128)}, f32[12,512]{1,0:T(8,128)S(1)}, f32[12,512]{1,0:T(8,128)}, f32[12,512]{1,0:T(8,128)}, f32[12,512]{1,0:T(8,128)S(1)}, ...), condition=%wide.region_5.6_spmd.clone, body=%wide.region_3.5_spmd.clone.sunk | while | flops 4982786 | bytes 32865 | solution.py:60
  194.5 48.7 %fusion.36 = (f32[2048]{0:T(1024)S(1)}, bf16[6144,2048]{1,0:T(8,128)(2,1)}, f32[2048]{0:T(1024)S(1)}) fusion(f32[6144,2048]{1,0:T(8,128)} %get-tuple-element.98, f32[2048]{0:T(1024)S(1)} %copy-done.6, f32[2048]{0:T(1024)S(1)} %copy-done.5, f32[6144]{0:T(1024)S(1)} %div.33), kind=kLoop, calls=%fused_computation.95 | loop fusion | flops 327151616 | bytes 75554816 | tf_op jit(solution)/shard_map/reduce_sum | solution.py:121
  243.2 12.9 %fusion.22 = f32[256,2048]{1,0:T(8,128)} fusion(bf16[6144,256]{1,0:T(8,128)(2,1)S(1)} %scatter_custom_fusion, bf16[6144,2048]{1,0:T(8,128)(2,1)} %get-tuple-element.74), kind=kOutput, calls=%fused_computation.37 | convolution fusion | flops 6442450944 | bytes 30408704 | tf_op jit(solution)/shard_map/dot_general | solution.py:115
  256.2 75.9 %all-reduce = (f32[2048]{0:T(1024)S(1)}, f32[2048]{0:T(1024)S(1)}) all-reduce(f32[2048]{0:T(1024)S(1)} %get-tuple-element.73, f32[2048]{0:T(1024)S(1)} %get-tuple-element.80), channel_id=1, replica_groups=mesh['dp'=16,'mp'=2] {'dp'}, use_global_device_ids=true, to_apply=%region_8.9 | all-reduce | flops 4096 | bytes 32768 | tf_op jit(solution)/shard_map/psum | solution.py:123
  332.8 49.9 %all-reduce.3.cloned.1.call-done = f32[256,2048]{1,0:T(8,128)} async-done(((f32[256,2048]{1,0:T(8,128)}), f32[256,2048]{1,0:T(8,128)}) %all-reduce.3.cloned.1.call-update) | async-done | bytes 2097168 | tf_op jit(solution)/shard_map/psum | solution.py:123
  382.6 6.6 %divide_subtract_fusion = (f32[256,2048]{1,0:T(8,128)}, f32[256,2048]{1,0:T(8,128)}, f32[256,2048]{1,0:T(8,128)}) fusion(f32[256,2048]{1,0:T(8,128)S(1)} %copy-done.2, f32[256,2048]{1,0:T(8,128)} %all-reduce.3.cloned.1.call-done, f32[256,2048]{1,0:T(8,128)} %param.26, f32[256,2048]{1,0:T(8,128)} %param.27), kind=kLoop, calls=%fused_computation.41 | loop fusion | flops 5767168 | bytes 14680064 | tf_op jit(solution)/shard_map/sub | solution.py:66
  (145 shorter events, 54.9 us)
Async XLA Ops:
  9.6 24.9 %all-to-all-start = ((s32[16,1,384]{2,1,0:T(1,128)}), s32[16,1,384]{2,1,0:T(1,128)}, u32[]{:S(2)}, u32[]{:S(2)}) async-start(s32[16,1,384]{2,1,0:T(1,128)} %compare_select_fusion.1), calls=%async_computation | async-start | bytes 49152 | tf_op jit(solution)/shard_map/all_to_all | solution.py:103
  17.9 364.7 %all-reduce.3.cloned.1.call-start = ((), (), s32[]{:S(2)}) async-start(), calls=%async_computation.1 | async-start | bytes 4194304 | tf_op jit(solution)/shard_map/psum | solution.py:123
  21.6 66.1 %copy-start.4 = (bf16[1,384,256]{2,1,0:T(8,128)(2,1)S(1)}, bf16[1,384,256]{2,1,0:T(8,128)(2,1)}, u32[]{:S(2)}) copy-start(bf16[1,384,256]{2,1,0:T(8,128)(2,1)} %get-tuple-element.85) | copy-start | bytes 589828
  21.6 72.2 %copy-start.3 = (bf16[1,384,256]{2,1,0:T(8,128)(2,1)S(1)}, bf16[1,384,256]{2,1,0:T(8,128)(2,1)}, u32[]{:S(2)}) copy-start(bf16[1,384,256]{2,1,0:T(8,128)(2,1)} %get-tuple-element.84) | copy-start | bytes 589828
  21.6 82.9 %collective-permute-start.14 = (bf16[1,384,256]{2,1,0:T(8,128)(2,1)S(1)}, bf16[1,384,256]{2,1,0:T(8,128)(2,1)S(1)}, u32[]{:S(2)}, u32[]{:S(2)}) collective-permute-start(bf16[1,384,256]{2,1,0:T(8,128)(2,1)S(1)} %get-tuple-element.81), channel_id=1, source_target_pairs={{0,30},{2,28},{4,26},{6,24},{8,22},{10,20},{12,18},{14,16},{16,14}... | collective-permute-start | bytes 589832 | tf_op jit(solution)/shard_map/ppermute | solution.py:28
  27.0 76.7 %collective-permute-start.13 = (bf16[1,384,256]{2,1,0:T(8,128)(2,1)S(1)}, bf16[1,384,256]{2,1,0:T(8,128)(2,1)S(1)}, u32[]{:S(2)}, u32[]{:S(2)}) collective-permute-start(bf16[1,384,256]{2,1,0:T(8,128)(2,1)S(1)} %get-tuple-element.82), channel_id=1, source_target_pairs={{0,28},{2,30},{4,24},{6,26},{8,20},{10,22},{12,16},{14,18},{16,12}... | collective-permute-start | bytes 589832 | tf_op jit(solution)/shard_map/ppermute | solution.py:28
  27.6 75.5 %collective-permute-start.12 = (bf16[1,384,256]{2,1,0:T(8,128)(2,1)}, bf16[1,384,256]{2,1,0:T(8,128)(2,1)S(1)}, u32[]{:S(2)}, u32[]{:S(2)}) collective-permute-start(bf16[1,384,256]{2,1,0:T(8,128)(2,1)} %get-tuple-element.83), channel_id=1, source_target_pairs={{0,26},{2,24},{4,30},{6,28},{8,18},{10,16},{12,22},{14,20},{16,10}... | collective-permute-start | bytes 589832 | tf_op jit(solution)/shard_map/ppermute | solution.py:28
  30.9 14.3 %collective-permute-start.1 = (bf16[1,384,256]{2,1,0:T(8,128)(2,1)}, bf16[1,384,256]{2,1,0:T(8,128)(2,1)S(1)}, u32[]{:S(2)}, u32[]{:S(2)}) collective-permute-start(bf16[1,384,256]{2,1,0:T(8,128)(2,1)} %get-tuple-element.94), channel_id=1, source_target_pairs={{0,4},{2,6},{4,0},{6,2},{8,12},{10,14},{12,8},{14,10},{16,20},{18,... | collective-permute-start | bytes 589832 | tf_op jit(solution)/shard_map/ppermute | solution.py:28
  32.3 10.8 %collective-permute-start = (bf16[1,384,256]{2,1,0:T(8,128)(2,1)}, bf16[1,384,256]{2,1,0:T(8,128)(2,1)S(1)}, u32[]{:S(2)}, u32[]{:S(2)}) collective-permute-start(bf16[1,384,256]{2,1,0:T(8,128)(2,1)} %get-tuple-element.95), channel_id=1, source_target_pairs={{0,2},{2,0},{4,6},{6,4},{8,10},{10,8},{12,14},{14,12},{16,18},{18,... | collective-permute-start | bytes 589832 | tf_op jit(solution)/shard_map/ppermute | solution.py:28
  43.1 9.0 %collective-permute-start.2 = (bf16[1,384,256]{2,1,0:T(8,128)(2,1)}, bf16[1,384,256]{2,1,0:T(8,128)(2,1)S(1)}, u32[]{:S(2)}, u32[]{:S(2)}) collective-permute-start(bf16[1,384,256]{2,1,0:T(8,128)(2,1)} %get-tuple-element.93), channel_id=1, source_target_pairs={{0,6},{2,4},{4,2},{6,0},{8,14},{10,12},{12,10},{14,8},{16,22},{18,... | collective-permute-start | bytes 589832 | tf_op jit(solution)/shard_map/ppermute | solution.py:28
  45.2 11.0 %collective-permute-start.3 = (bf16[1,384,256]{2,1,0:T(8,128)(2,1)}, bf16[1,384,256]{2,1,0:T(8,128)(2,1)S(1)}, u32[]{:S(2)}, u32[]{:S(2)}) collective-permute-start(bf16[1,384,256]{2,1,0:T(8,128)(2,1)} %get-tuple-element.92), channel_id=1, source_target_pairs={{0,8},{2,10},{4,12},{6,14},{8,0},{10,2},{12,4},{14,6},{16,24},{18,... | collective-permute-start | bytes 589832 | tf_op jit(solution)/shard_map/ppermute | solution.py:28
  52.1 9.5 %collective-permute-start.4 = (bf16[1,384,256]{2,1,0:T(8,128)(2,1)}, bf16[1,384,256]{2,1,0:T(8,128)(2,1)S(1)}, u32[]{:S(2)}, u32[]{:S(2)}) collective-permute-start(bf16[1,384,256]{2,1,0:T(8,128)(2,1)} %get-tuple-element.91), channel_id=1, source_target_pairs={{0,10},{2,8},{4,14},{6,12},{8,2},{10,0},{12,6},{14,4},{16,26},{18,... | collective-permute-start | bytes 589832 | tf_op jit(solution)/shard_map/ppermute | solution.py:28
  56.2 7.7 %collective-permute-start.5 = (bf16[1,384,256]{2,1,0:T(8,128)(2,1)}, bf16[1,384,256]{2,1,0:T(8,128)(2,1)S(1)}, u32[]{:S(2)}, u32[]{:S(2)}) collective-permute-start(bf16[1,384,256]{2,1,0:T(8,128)(2,1)} %get-tuple-element.90), channel_id=1, source_target_pairs={{0,12},{2,14},{4,8},{6,10},{8,4},{10,6},{12,0},{14,2},{16,28},{18,... | collective-permute-start | bytes 589832 | tf_op jit(solution)/shard_map/ppermute | solution.py:28
  61.6 9.3 %collective-permute-start.6 = (bf16[1,384,256]{2,1,0:T(8,128)(2,1)}, bf16[1,384,256]{2,1,0:T(8,128)(2,1)S(1)}, u32[]{:S(2)}, u32[]{:S(2)}) collective-permute-start(bf16[1,384,256]{2,1,0:T(8,128)(2,1)} %get-tuple-element.89), channel_id=1, source_target_pairs={{0,14},{2,12},{4,10},{6,8},{8,6},{10,4},{12,2},{14,0},{16,30},{18,... | collective-permute-start | bytes 589832 | tf_op jit(solution)/shard_map/ppermute | solution.py:28
  63.9 13.2 %collective-permute-start.7 = (bf16[1,384,256]{2,1,0:T(8,128)(2,1)}, bf16[1,384,256]{2,1,0:T(8,128)(2,1)S(1)}, u32[]{:S(2)}, u32[]{:S(2)}) collective-permute-start(bf16[1,384,256]{2,1,0:T(8,128)(2,1)} %get-tuple-element.88), channel_id=1, source_target_pairs={{0,16},{2,18},{4,20},{6,22},{8,24},{10,26},{12,28},{14,30},{16,0},... | collective-permute-start | bytes 589832 | tf_op jit(solution)/shard_map/ppermute | solution.py:28
  71.0 16.7 %collective-permute-start.8 = (bf16[1,384,256]{2,1,0:T(8,128)(2,1)}, bf16[1,384,256]{2,1,0:T(8,128)(2,1)S(1)}, u32[]{:S(2)}, u32[]{:S(2)}) collective-permute-start(bf16[1,384,256]{2,1,0:T(8,128)(2,1)} %get-tuple-element.87), channel_id=1, source_target_pairs={{0,18},{2,16},{4,22},{6,20},{8,26},{10,24},{12,30},{14,28},{16,2},... | collective-permute-start | bytes 589832 | tf_op jit(solution)/shard_map/ppermute | solution.py:28
  77.1 16.6 %collective-permute-start.9 = (bf16[1,384,256]{2,1,0:T(8,128)(2,1)}, bf16[1,384,256]{2,1,0:T(8,128)(2,1)S(1)}, u32[]{:S(2)}, u32[]{:S(2)}) collective-permute-start(bf16[1,384,256]{2,1,0:T(8,128)(2,1)} %get-tuple-element.86), channel_id=1, source_target_pairs={{0,20},{2,22},{4,16},{6,18},{8,28},{10,30},{12,24},{14,26},{16,4},... | collective-permute-start | bytes 589832 | tf_op jit(solution)/shard_map/ppermute | solution.py:28
  87.7 11.6 %collective-permute-start.10 = (bf16[1,384,256]{2,1,0:T(8,128)(2,1)S(1)}, bf16[1,384,256]{2,1,0:T(8,128)(2,1)S(1)}, u32[]{:S(2)}, u32[]{:S(2)}) collective-permute-start(bf16[1,384,256]{2,1,0:T(8,128)(2,1)S(1)} %copy-done.4), channel_id=1, source_target_pairs={{0,22},{2,20},{4,18},{6,16},{8,30},{10,28},{12,26},{14,24},{16,6},... | collective-permute-start | bytes 589832 | tf_op jit(solution)/shard_map/ppermute | solution.py:28
  93.7 8.7 %collective-permute-start.11 = (bf16[1,384,256]{2,1,0:T(8,128)(2,1)S(1)}, bf16[1,384,256]{2,1,0:T(8,128)(2,1)S(1)}, u32[]{:S(2)}, u32[]{:S(2)}) collective-permute-start(bf16[1,384,256]{2,1,0:T(8,128)(2,1)S(1)} %copy-done.3), channel_id=1, source_target_pairs={{0,24},{2,26},{4,28},{6,30},{8,16},{10,18},{12,20},{14,22},{16,8},... | collective-permute-start | bytes 589832 | tf_op jit(solution)/shard_map/ppermute | solution.py:28
  243.2 89.0 %copy-start.9 = (f32[2048]{0:T(1024)S(1)}, f32[2048]{0:T(1024)}, u32[]{:S(2)}) copy-start(f32[2048]{0:T(1024)} %param.30) | copy-start | bytes 24580
  243.2 89.0 %copy-start.10 = (f32[2048]{0:T(1024)S(1)}, f32[2048]{0:T(1024)}, u32[]{:S(2)}) copy-start(f32[2048]{0:T(1024)} %param.31) | copy-start | bytes 24580
  243.2 88.9 %copy-start.11 = (f32[2048]{0:T(1024)S(1)}, f32[2048]{0:T(1024)}, u32[]{:S(2)}) copy-start(f32[2048]{0:T(1024)} %param.29) | copy-start | bytes 24580
  243.2 88.9 %copy-start.12 = (f32[2048]{0:T(1024)S(1)}, f32[2048]{0:T(1024)}, u32[]{:S(2)}) copy-start(f32[2048]{0:T(1024)} %param.28) | copy-start | bytes 24580
  256.2 126.5 %copy-start.2 = (f32[256,2048]{1,0:T(8,128)S(1)}, f32[256,2048]{1,0:T(8,128)}, u32[]{:S(2)}) copy-start(f32[256,2048]{1,0:T(8,128)} %param.23) | copy-start | bytes 6291460
  (7 other events, 218.7 us)
Sparse Core Ops, SparseCore 0:
  256.3 126.2 all-reduce.2
